TPU v7x, 256 devices: a whole 4x4x8 slice. The times are simulated.
256 devices in a mesh: row: 8 (over y, core), col: 32 (over z, x).
Axes of the slice: x: 4, y: 4, z: 8, core: 2. Of those that a mesh axis runs over, the one named last changes fastest.
Arguments:
- diag_block: float32 [1024, 1024], P('row')
- panel: bfloat16 [64, 1024, 1024], P('col', 'row'), may hold values from -1 to 1
- trailing: bfloat16 [32, 12, 1024, 1024], P('col', None, 'row'), may hold values from -6 to 6
- slot_rows: int32 [32, 12], replicated, may hold values from -1 to 63, as said below
- slot_cols: int32 [32, 12], replicated, may hold values from 0 to 1, as said below
Outputs:
- panel_factor: bfloat16 [64, 1024, 1024], P('col', 'row')
- updated: bfloat16 [32, 12, 1024, 1024], P('col', None, 'row')
Inputs may be any that keep to these rules, and one draw needn't show every extreme that they name: Slot s of grid column c holds the tile at tile row slot_rows[c, s] and tile column 2 * c + slot_cols[c, s] of the trailing matrix, or nothing where slot_rows[c, s] is -1. Live slots come first in each column; the pairs of one column are distinct and lie on or below the diagonal (tile row at least tile column). Within one grid column, live slots whose tile rows a and a' have a // 2 == a' // 2 have a == a'. Every column holds at least one live slot, column 0 fills all 12 slots and column 16 holds exactly one. `slot_cols`: 0 in empty slots.
All inputs are finite; a program needn't handle non-finite values.
Results may differ from a plain program's by a relative error of at most 0.0019.
Values may be sent and summed in bfloat16 or wider, within the bound.
No kernel may reach another device: no remote copies, remote signals or barrier semaphores. Data moves between devices by JAX's collectives and lax.ppermute only.
A program may use at most 128 MiB of HBM per device.

v0:
```python
import jax
import jax.numpy as jnp
from jax import lax
from jax.sharding import PartitionSpec as P


def slot_product(slices, left_ids, source_tiles, col_ids, position):
    left_slice = lax.dynamic_index_in_dim(slices, left_ids[position], 0, keepdims=False)
    right_tile = lax.dynamic_index_in_dim(source_tiles, col_ids[position], 0, keepdims=False)
    return lax.dot_general(
        left_slice, right_tile, (((1,), (1,)), ((), ())), preferred_element_type=jnp.float32
    )


def subtract_slot(buffer, position, update):
    previous = lax.dynamic_index_in_dim(buffer, position, 0, keepdims=False).astype(jnp.float32)
    return lax.dynamic_update_index_in_dim(
        buffer, (previous - update).astype(jnp.bfloat16), position, 0
    )


def local(diag_block, panel, trailing, slot_rows, slot_cols):
    diag_full = lax.all_gather(diag_block, "row", axis=0, tiled=True)
    factor = jnp.linalg.cholesky(diag_full)
    tile_count, row_count, tile_width = panel.shape
    stacked = panel.astype(jnp.float32).reshape(tile_count * row_count, tile_width)
    solved = lax.linalg.triangular_solve(factor, stacked.T, left_side=True, lower=True)
    panel_factor = solved.T.reshape(tile_count, row_count, tile_width).astype(jnp.bfloat16)
    whole_tiles = lax.all_gather(panel_factor, "row", axis=1, tiled=True)
    column_index = lax.axis_index("col")
    own_rows = lax.dynamic_index_in_dim(slot_rows, column_index, 0, keepdims=False)
    own_cols = lax.dynamic_index_in_dim(slot_cols, column_index, 0, keepdims=False)
    own_count = jnp.sum((own_rows >= 0).astype(jnp.int32))
    slices = lax.all_gather(panel_factor, "col", axis=0, tiled=True)

    def own_step(position, buffer):
        return subtract_slot(
            buffer, position, slot_product(slices, own_rows, whole_tiles, own_cols, position)
        )

    buffer = lax.fori_loop(0, own_count, own_step, trailing[0])
    return (panel_factor, buffer[None])


def solution(mesh):
    return jax.shard_map(
        local,
        mesh=mesh,
        in_specs=(P("row", None), P("col", "row", None), P("col", None, "row", None), P(), P()),
        out_specs=(P("col", "row", None), P("col", None, "row", None)),
        check_vma=False,
    )
```

profile of v0, /device:TPU:1, one launch (start us, length us, event | category | flops | bytes accessed | tf_op | source)
XLA Modules:
  0.0 681.8 jit_solution(6531067428901336610)
XLA Ops:
  9.6 43.7 %all-gather.4.cloned.1.call-done = f32[1024,1024]{0,1:T(8,128)} async-done(((f32[128,1024]{0,1:T(8,128)}), f32[1024,1024]{0,1:T(8,128)}) %all-gather.4.cloned.1.call-update) | async-done | bytes 4194320 | tf_op jit(solution)/shard_map/all_gather | solution.py:23
  53.3 5.3 copy.18
  58.7 4.4 fusion.18
  65.0 11.7 %cholesky.223 = f32[128,128]{1,0:T(8,128)S(1)} custom-call(f32[128,128]{1,0:T(8,128)S(1)} %cholesky.580), custom_call_target="Cholesky" | custom-call | tf_op jit(solution)/shard_map/jit(cholesky)/cholesky | solution.py:24
  76.8 9.8 %custom-call.62 = f32[1,128,128]{1,2,0:T(8,128)S(1)} custom-call(f32[1,128,128]{2,1,0:T(8,128)S(1)} %get-tuple-element.117), custom_call_target="InvertDiagBlocksLowerTriangular" | custom-call | tf_op jit(solution)/shard_map/jit(cholesky)/cholesky | solution.py:24
  93.0 12.2 %cholesky.244 = f32[128,128]{1,0:T(8,128)S(1)} custom-call(f32[128,128]{1,0:T(8,128)S(1)} %cholesky.584), custom_call_target="Cholesky" | custom-call | tf_op jit(solution)/shard_map/jit(cholesky)/cholesky | solution.py:24
  105.8 9.8 %custom-call.63 = f32[1,128,128]{1,2,0:T(8,128)S(1)} custom-call(f32[1,128,128]{2,1,0:T(8,128)S(1)} %get-tuple-element.114), custom_call_target="InvertDiagBlocksLowerTriangular" | custom-call | tf_op jit(solution)/shard_map/jit(cholesky)/cholesky | solution.py:24
  119.0 11.7 %cholesky.468 = f32[128,128]{1,0:T(8,128)S(1)} custom-call(f32[128,128]{1,0:T(8,128)S(1)} %cholesky.589), custom_call_target="Cholesky" | custom-call | tf_op jit(solution)/shard_map/jit(cholesky)/cholesky | solution.py:24
  132.0 9.8 %custom-call.64 = f32[1,128,128]{1,2,0:T(8,128)S(1)} custom-call(f32[1,128,128]{2,1,0:T(8,128)S(1)} %get-tuple-element.111), custom_call_target="InvertDiagBlocksLowerTriangular" | custom-call | tf_op jit(solution)/shard_map/jit(cholesky)/cholesky | solution.py:24
  145.3 11.8 %cholesky.487 = f32[128,128]{1,0:T(8,128)S(1)} custom-call(f32[128,128]{1,0:T(8,128)S(1)} %cholesky.594), custom_call_target="Cholesky" | custom-call | tf_op jit(solution)/shard_map/jit(cholesky)/cholesky | solution.py:24
  158.5 9.8 %custom-call.65 = f32[1,128,128]{1,2,0:T(8,128)S(1)} custom-call(f32[1,128,128]{2,1,0:T(8,128)S(1)} %get-tuple-element.108), custom_call_target="InvertDiagBlocksLowerTriangular" | custom-call | tf_op jit(solution)/shard_map/jit(cholesky)/cholesky | solution.py:24
  171.7 11.7 %cholesky.506 = f32[128,128]{1,0:T(8,128)S(1)} custom-call(f32[128,128]{1,0:T(8,128)S(1)} %cholesky.599), custom_call_target="Cholesky" | custom-call | tf_op jit(solution)/shard_map/jit(cholesky)/cholesky | solution.py:24
  184.7 10.0 %custom-call.66 = f32[1,128,128]{1,2,0:T(8,128)S(1)} custom-call(f32[1,128,128]{2,1,0:T(8,128)S(1)} %get-tuple-element.105), custom_call_target="InvertDiagBlocksLowerTriangular" | custom-call | tf_op jit(solution)/shard_map/jit(cholesky)/cholesky | solution.py:24
  198.1 11.7 %cholesky.526 = f32[128,128]{1,0:T(8,128)S(1)} custom-call(f32[128,128]{1,0:T(8,128)S(1)} %cholesky.604), custom_call_target="Cholesky" | custom-call | tf_op jit(solution)/shard_map/jit(cholesky)/cholesky | solution.py:24
  211.0 9.8 %custom-call.67 = f32[1,128,128]{1,2,0:T(8,128)S(1)} custom-call(f32[1,128,128]{2,1,0:T(8,128)S(1)} %get-tuple-element.102), custom_call_target="InvertDiagBlocksLowerTriangular" | custom-call | tf_op jit(solution)/shard_map/jit(cholesky)/cholesky | solution.py:24
  223.8 12.1 %cholesky.546 = f32[128,128]{1,0:T(8,128)S(1)} custom-call(f32[128,128]{1,0:T(8,128)S(1)} %cholesky.609), custom_call_target="Cholesky" | custom-call | tf_op jit(solution)/shard_map/jit(cholesky)/cholesky | solution.py:24
  237.2 9.8 %custom-call.68 = f32[1,128,128]{1,2,0:T(8,128)S(1)} custom-call(f32[1,128,128]{2,1,0:T(8,128)S(1)} %get-tuple-element.99), custom_call_target="InvertDiagBlocksLowerTriangular" | custom-call | tf_op jit(solution)/shard_map/jit(cholesky)/cholesky | solution.py:24
  249.7 11.7 %cholesky.564 = f32[128,128]{1,0:T(8,128)S(1)} custom-call(f32[128,128]{1,0:T(8,128)S(1)} %convolution_subtract_fusion.13), custom_call_target="Cholesky" | custom-call | tf_op jit(solution)/shard_map/jit(cholesky)/cholesky | solution.py:24
  268.3 4.8 select_select_fusion
  273.1 23.0 %while.12 = (s32[]{:T(128)}, f32[1024,1024]{1,0:T(8,128)}, s32[8,2]{0,1:T(2,128)S(1)}, f32[8,128,128]{2,1,0:T(8,128)S(1)}, s32[]{:T(128)}) while((s32[]{:T(128)}, f32[1024,1024]{1,0:T(8,128)}, s32[8,2]{0,1:T(2,128)S(1)}, f32[8,128,128]{2,1,0:T(8,128)S(1)}, s32[]{:T(128)}) %tuple.74), condition=%wide.while_cond, body=%wide.while_body.sunk | while | flops 2 | bytes 131189 | solution.py:27
  296.1 78.8 %custom-call.69 = f32[8,128,128]{1,2,0:T(8,128)S(1)} custom-call(f32[8,128,128]{2,1,0:T(8,128)S(1)} %get-tuple-element.48), custom_call_target="InvertDiagBlocksLowerTriangular" | custom-call | tf_op jit(solution)/shard_map/triangular_solve | solution.py:27
  398.6 34.2 %all-gather.8.cloned.1.call-done = bf16[2,1024,1024]{2,1,0:T(8,128)(2,1)} async-done(((bf16[2,128,1024]{2,1,0:T(8,128)(2,1)}), bf16[2,1024,1024]{2,1,0:T(8,128)(2,1)}) %all-gather.8.cloned.1.call-update) | async-done | bytes 4194320 | tf_op jit(solution)/shard_map/all_gather | solution.py:29
  432.8 142.9 %all-gather.6.cloned.1.call-done = bf16[64,128,1024]{2,1,0:T(8,128)(2,1)} async-done(((bf16[2,128,1024]{2,1,0:T(8,128)(2,1)}), bf16[64,128,1024]{2,1,0:T(8,128)(2,1)}) %all-gather.6.cloned.1.call-update) | async-done | bytes 16777232 | tf_op jit(solution)/shard_map/all_gather | solution.py:34
  575.8 97.6 %while.11 = (s32[]{:T(128)}, bf16[12,128,1024]{2,1,0:T(8,128)(2,1)S(1)}, s32[]{:T(128)}, s32[12]{0:T(128)S(1)}, bf16[64,128,1024]{2,1,0:T(8,128)(2,1)}, /*index=...) while((s32[]{:T(128)}, ...), condition=%wide.region_18.19_spmd, body=%wide.region_17.18_spmd.sunk | while | flops 268828672 | bytes 3408139 | solution.py:41
  (164 shorter events, 132.0 us)
Async XLA Ops:
  7.2 1.0 copy-start.4
  7.2 2.1 copy-start.5
  7.2 46.1 %all-gather.4.cloned.1.call-start = ((), (), s32[]{:S(2)}) async-start(), calls=%async_computation | async-start | bytes 4718592 | tf_op jit(solution)/shard_map/all_gather | solution.py:23
  9.2 423.6 %all-gather.8.cloned.1.call-start = ((), (), s32[]{:S(2)}) async-start(), calls=%async_computation.2 | async-start | bytes 4718592 | tf_op jit(solution)/shard_map/all_gather | solution.py:29
  9.6 372.6 %copy-start.3 = (f32[1024,256]{1,0:T(8,128)}, f32[1024,256]{1,0:T(8,128)S(1)}, u32[]{:S(2)}) copy-start(f32[1024,256]{1,0:T(8,128)S(1)} %bitcast_convert_fusion) | copy-start | bytes 3145732
  63.1 1.9 copy-start
  374.9 9.7 %copy-start.6 = (f32[8,128,128]{1,2,0:T(8,128)}, f32[8,128,128]{1,2,0:T(8,128)S(1)}, u32[]{:S(2)}) copy-start(f32[8,128,128]{1,2,0:T(8,128)S(1)} %custom-call.69) | copy-start | bytes 1572868
  384.7 13.1 %copy-start.7 = (s32[32,12]{0,1:T(8,128)S(1)}, s32[32,12]{0,1:T(8,128)}, u32[]{:S(2)}) copy-start(s32[32,12]{0,1:T(8,128)} %param.11) | copy-start | bytes 4612
  384.7 13.1 %copy-start.8 = (s32[32,12]{0,1:T(8,128)S(1)}, s32[32,12]{0,1:T(8,128)}, u32[]{:S(2)}) copy-start(s32[32,12]{0,1:T(8,128)} %param.10) | copy-start | bytes 4612
  384.7 191.1 %copy-start.2 = (bf16[1,12,128,1024]{3,2,1,0:T(8,128)(2,1)S(1)}, bf16[1,12,128,1024]{3,2,1,0:T(8,128)(2,1)}, u32[]{:S(2)}) copy-start(bf16[1,12,128,1024]{3,2,1,0:T(8,128)(2,1)} %param.9) | copy-start | bytes 9437188
  397.0 178.7 %all-gather.6.cloned.1.call-start = ((), (), s32[]{:S(2)}) async-start(), calls=%async_computation.1 | async-start | bytes 17301504 | tf_op jit(solution)/shard_map/all_gather | solution.py:34
  673.4 1.7 copy-start.1
Sparse Core Ops, SparseCore 0:
  10.4 42.8 all-gather.3
  397.1 35.6 all-gather.7
  436.0 139.6 all-gather.5
where the time goes:
time: 693 us; the launch traced here: 682 us
  other arithmetic  261 us (38%)
  waiting for transfers between devices  222 us (32%)
  matrix products  73.2 us (11%)
  local copies, waits for them, and re-layouts  53.5 us (8%)
  loops' own time  52.9 us (8%)
  between operations  19.3 us (3%)
    another operation x30, other arithmetic, local(): factor = jnp.linalg.cholesky(diag_full)  173 us
    all_gather x1, waiting for transfers between devices, local(): slices = lax.all_gather(panel_factor, 'col', axis=0, tiled=True)  143 us
    another operation x3, other arithmetic, local(): lax.linalg.triangular_solve(factor, stacked.T, left_side=True, lower=True)  83.6 us
    another operation x1, loops' own time, local(): buffer = lax.fori_loop(0, own_count, own_step, trailing[0])  52.7 us
    all_gather x1, waiting for transfers between devices, local(): diag_full = lax.all_gather(diag_block, 'row', axis=0, tiled=True)  43.7 us
    all_gather x1, waiting for transfers between devices, local(): whole_tiles = lax.all_gather(panel_factor, 'row', axis=1, tiled=True)  34.2 us
    dot_general x12, matrix products, slot_product(): lax.dot_general(left_slice, right_tile, (((1,), (1,)), ((), ())), preferr...  30.3 us
    another operation x14, matrix products, local(): factor = jnp.linalg.cholesky(diag_full)  23.1 us
  transfers between devices with their start and end apart: 3, of which 3 were waited for; matrix products, arithmetic and copies ran while one was open for 0% of the time, Pallas kernels for 0%

commit v1 on v0

v1 whole, which is shorter than its diff:
```python
import jax
import jax.numpy as jnp
from jax import lax
from jax.experimental import pallas as pl
from jax.experimental.pallas import tpu as pltpu
from jax.sharding import PartitionSpec as P

HIGHEST = lax.Precision.HIGHEST
F32, BF16 = jnp.float32, jnp.bfloat16
B = 128


def lane_splat(x, lane):
    return jnp.broadcast_to(x[:, lane:lane + 1], (8, B))


def row_splat(x, row):
    return jnp.broadcast_to(x[row:row + 1, :], (8, B))


def tree_sum(terms):
    terms = list(terms)
    while len(terms) > 1:
        terms = [terms[i] + terms[i + 1] for i in range(0, len(terms), 2)]
    return terms[0]


def inverse_factor(block, out):
    sub = lax.broadcasted_iota(jnp.int32, (8, B), 0)
    lane = lax.broadcasted_iota(jnp.int32, (8, B), 1)
    rows = [block[8 * g:8 * g + 8, :] for g in range(16)]
    ones = [jnp.where(lane == sub + 8 * g, 1.0, 0.0).astype(F32) for g in range(16)]
    for g in range(16):
        left, right = rows[g], ones[g]
        cols = [lane_splat(left, 8 * g + k) for k in range(8)]
        done = jnp.zeros((8, B), F32)
        for k in range(8):
            here = sub == k
            pivot = row_splat(cols[k], k)
            recip = 1.0 / pivot
            right_row = row_splat(right, k)
            done = jnp.where(here, right_row * lax.rsqrt(pivot), done)
            left_row = row_splat(left, k) * recip
            right_row = right_row * recip
            for m in range(k + 1, 8):
                entry = row_splat(cols[m], k) * recip
                cols[m] = jnp.where(here, entry, cols[m] - cols[k] * entry)
            left = jnp.where(here, left_row, left - cols[k] * left_row)
            right = jnp.where(here, right_row, right - cols[k] * right_row)
        out[8 * g:8 * g + 8, :] = done
        if g < 15:
            left_rows = [row_splat(left, k) for k in range(8)]
            right_rows = [row_splat(right, k) for k in range(8)]
            for h in range(g + 1, 16):
                coefs = [lane_splat(rows[h], 8 * g + k) for k in range(8)]
                rows[h] = rows[h] - tree_sum(coefs[k] * left_rows[k] for k in range(8))
                ones[h] = ones[h] - tree_sum(coefs[k] * right_rows[k] for k in range(8))


def dot(a, b, contract, precision=None):
    return lax.dot_general(a, b, ((contract[0], contract[1]), ((), ())), precision=precision, preferred_element_type=F32)


def factor_kernel(ranks, *refs):
    parts, (high, low), (work, diag_inverse) = refs[:8], refs[8:10], refs[10:]
    for q in range(8):
        work[pl.ds(pl.multiple_of(ranks[q] * B, B), B), :] = parts[q][...]

    def step(j, carry):
        o = pl.multiple_of(j * B, B)
        inverse_factor(work[pl.ds(o, B), pl.ds(o, B)], diag_inverse)

        def update(j):
            def run():
                s, e = j * B, j * B + B
                inv = diag_inverse[...]
                if j:
                    work[s:e, :s] = dot(inv, work[s:e, :s], ((1,), (0,)), HIGHEST)
                work[s:e, s:e] = inv
                if j < 7:
                    work[s:e, e:] = dot(inv, work[s:e, e:], ((1,), (0,)), HIGHEST)
                for i in range(j + 1, 8):
                    t, u = i * B, i * B + B
                    coef = work[s:e, t:u]
                    if j:
                        work[t:u, :s] -= dot(coef, work[s:e, :s], ((0,), (0,)), HIGHEST)
                    work[t:u, s:e] = -dot(coef, work[s:e, s:e], ((0,), (0,)), HIGHEST)
                    work[t:u, t:] -= dot(coef, work[s:e, t:], ((0,), (0,)), HIGHEST)
            return run

        lax.switch(j, [update(j) for j in range(8)])
        return carry

    lax.fori_loop(0, 8, step, 0)
    for j in range(8):
        s, e = j * B, j * B + B
        whole = work[s:e, :e]
        top = whole.astype(BF16)
        high[s:e, :e] = top
        low[s:e, :e] = (whole - top.astype(F32)).astype(BF16)
        if e < 1024:
            high[s:e, e:] = jnp.zeros((B, 1024 - e), BF16)
            low[s:e, e:] = jnp.zeros((B, 1024 - e), BF16)


def inverse_parts(ranks, parts):
    vmem = pl.BlockSpec(memory_space=pltpu.VMEM)
    half = jax.ShapeDtypeStruct((1024, 1024), BF16)
    return pl.pallas_call(
        factor_kernel,
        out_shape=(half, half),
        in_specs=[pl.BlockSpec(memory_space=pltpu.SMEM)] + [vmem] * 8,
        out_specs=(vmem, vmem),
        scratch_shapes=[pltpu.VMEM((1024, 1024), F32), pltpu.VMEM((B, B), F32)],
        compiler_params=pltpu.CompilerParams(vmem_limit_bytes=40 << 20),
        cost_estimate=pl.CostEstimate(flops=20_000_000_000, bytes_accessed=100_000_000, transcendentals=0),
        name="factor",
    )(ranks, *parts)


def solve_rows(raw, high, low):
    pieces = []
    for n in range(4):
        s, e = 256 * n, 256 * n + 256
        left = raw[:, :e]
        piece = dot(left, low[s:e, :e], ((1,), (1,))) + dot(left, high[s:e, :e], ((1,), (1,)))
        pieces.append(piece.astype(BF16))
    return jnp.concatenate(pieces, axis=1)


def own_kernel(ranks, raw, high, low, out):
    solved = solve_rows(raw[...].reshape(2 * B, 1024), high, low)
    out[...] = solved.reshape(2, B, 1024)


def solve_own(ranks, raw, high, low):
    whole = pl.BlockSpec((1024, 1024), lambda q, r: (0, 0))
    return pl.pallas_call(
        own_kernel,
        out_shape=jax.ShapeDtypeStruct((2, 1024, 1024), BF16),
        grid_spec=pltpu.PrefetchScalarGridSpec(
            num_scalar_prefetch=1,
            grid=(8,),
            in_specs=[pl.BlockSpec((None, 2, B, 1024), lambda q, r: (q, 0, 0, 0)), whole, whole],
            out_specs=pl.BlockSpec((2, B, 1024), lambda q, r: (0, r[q], 0)),
        ),
        compiler_params=pltpu.CompilerParams(vmem_limit_bytes=32 << 20),
        cost_estimate=pl.CostEstimate(flops=6_000_000_000, bytes_accessed=12_000_000, transcendentals=0),
        name="own",
    )(ranks, raw, high, low)


def slot_kernel(table, raw, high, low, tiles, trailing, out):
    s = pl.program_id(0)

    @pl.when(table[2, s] > 0)
    def _():
        left = solve_rows(raw[...], high, low)
        product = dot(left, tiles[table[1, s]], ((1,), (1,)))
        out[...] = (trailing[...].astype(F32) - product).astype(BF16)

    @pl.when(table[2, s] == 0)
    def _():
        out[...] = trailing[...]


def update_slots(table, slices, high, low, tiles, trailing):
    whole = pl.BlockSpec((1024, 1024), lambda s, t: (0, 0))
    slot = pl.BlockSpec((None, B, 1024), lambda s, t: (s, 0, 0))
    return pl.pallas_call(
        slot_kernel,
        out_shape=jax.ShapeDtypeStruct((12, B, 1024), BF16),
        grid_spec=pltpu.PrefetchScalarGridSpec(
            num_scalar_prefetch=1,
            grid=(12,),
            in_specs=[
                pl.BlockSpec((None, B, 1024), lambda s, t: (t[0, s], 0, 0)),
                whole,
                whole,
                pl.BlockSpec((2, 1024, 1024), lambda s, t: (0, 0, 0)),
                slot,
            ],
            out_specs=slot,
        ),
        compiler_params=pltpu.CompilerParams(vmem_limit_bytes=40 << 20),
        cost_estimate=pl.CostEstimate(flops=8_000_000_000, bytes_accessed=18_000_000, transcendentals=0),
        name="slots",
    )(table, slices, high, low, tiles, trailing)


def shift_y(x, k):
    return lax.ppermute(x, "row", [(r, (r + 2 * k) % 8) for r in range(8)])


def other_core(x):
    return lax.ppermute(x, "row", [(r, r ^ 1) for r in range(8)])


def row_parts(x):
    same = [x, shift_y(x, 1), shift_y(x, 3), shift_y(x, 2)]
    return same + [other_core(p) for p in same]


def local(diag_block, panel, trailing, slot_rows, slot_cols):
    row, col = lax.axis_index("row"), lax.axis_index("col")
    shifts = jnp.array([0, 1, 3, 2], jnp.int32)
    ranks = jnp.concatenate([(row - 2 * shifts) % 8, ((row ^ 1) - 2 * shifts) % 8]).astype(jnp.int32)
    wanted = jnp.any(slot_rows.reshape(1, -1) == jnp.arange(64, dtype=jnp.int32)[:, None], axis=1).reshape(32, 2)
    both = wanted[:, 0] & wanted[:, 1]
    first = jnp.where(wanted[:, 0], 0, 1)
    mine = lax.dynamic_index_in_dim(panel, first[col], 0, keepdims=False)
    slices = lax.all_gather(mine, "col", axis=0, tiled=False)

    high, low = inverse_parts(ranks, row_parts(diag_block))
    tiles = solve_own(ranks, jnp.stack(row_parts(panel)), high, low)
    panel_factor = lax.dynamic_slice_in_dim(tiles, row * B, B, axis=1)

    rows = lax.dynamic_index_in_dim(slot_rows, col, 0, keepdims=False)
    cols = lax.dynamic_index_in_dim(slot_cols, col, 0, keepdims=False)
    live = rows >= 0
    owner = jnp.maximum(rows, 0) // 2
    second = both[owner] & (rows % 2 == 1)
    table = jnp.stack([owner + 32 * (second & live), cols, live.astype(jnp.int32)])

    def one_tile(slices):
        return update_slots(table, slices, high, low, tiles, trailing[0])

    def two_tiles(slices):
        more = lax.all_gather(panel[1], "col", axis=0, tiled=False)
        return update_slots(table, jnp.concatenate([slices, more]), high, low, tiles, trailing[0])

    updated = lax.cond(jnp.any(both), two_tiles, one_tile, slices)
    return (panel_factor, updated[None])


def solution(mesh):
    return jax.shard_map(
        local,
        mesh=mesh,
        in_specs=(P("row", None), P("col", "row", None), P("col", None, "row", None), P(), P()),
        out_specs=(P("col", "row", None), P("col", None, "row", None)),
        check_vma=False,
    )
```

time: 693 us -> 287 us (0.41); the launches traced: 682 us -> 286 us
  other arithmetic: 261 us -> 17.6 us
  Pallas kernels: 0 us -> 86 us
  waiting for transfers between devices: 222 us -> 144 us
  matrix products: 73.2 us -> 0 us
  loops' own time: 52.9 us -> 0.03 us
  local copies, waits for them, and re-layouts: 53.5 us -> 8.54 us
  starting transfers between devices: 0.12 us -> 13.6 us
    another operation x33 -> x1, other arithmetic: 256 us -> 0.01 us  [local(): jnp.stack([owner + 32 * (second & live), cols, live.astype(jnp.int32)])]
    all_gather x3 -> x2, waiting for transfers between devices: 221 us -> 103 us  [the longest x1 103 us: two_tiles(): more = lax.all_gather(panel[1], 'col', axis=0, tiled=False)]
    pallas_call x0 -> x3, Pallas kernels: none -> 86 us  [the longest x1 52.3 us: inverse_parts(): pl.pallas_call(factor_kernel, out_shape=(half, half), in_specs=[pl.BlockS...]
    another operation x2 -> x1, loops' own time: 52.9 us -> 0.03 us  [local(): updated = lax.cond(jnp.any(both), two_tiles, one_tile, slices)]
    another operation x29 -> x0, matrix products: 42.8 us -> none  [the longest x14 23.1 us: local(): factor = jnp.linalg.cholesky(diag_full)]
    ppermute x0 -> x14, waiting for transfers between devices: none -> 41.1 us  [the longest x6 38.7 us: shift_y(): return lax.ppermute(x, 'row', [(r, (r + 2 * k) % 8) for r in range(8)])]
    dot_general x12 -> x0, matrix products: 30.3 us -> none  [slot_product(): lax.dot_general(left_slice, right_tile, (((1,), (1,)), ((), ())), preferr...]
    another operation x34 -> x1, local copies, waits for them, and re-layouts: 25.4 us -> 0.04 us  [local(): tiles = solve_own(ranks, jnp.stack(row_parts(panel)), high, low)]
  transfers between devices with their start and end apart: 3 -> 16, of which waited for: 3 -> 7; matrix products, arithmetic and copies ran while one was open for 0% -> 1% of each run, Pallas kernels for 0% -> 21%
where the time goes in v1:
time: 287 us; the launch traced here: 286 us
  waiting for transfers between devices  144 us (50%)
  Pallas kernels  86 us (30%)
  other arithmetic  17.6 us (6%)
  between operations  16.8 us (6%)
  starting transfers between devices  13.6 us (5%)
  local copies, waits for them, and re-layouts  8.54 us (3%)
    all_gather x1, waiting for transfers between devices, two_tiles(): more = lax.all_gather(panel[1], 'col', axis=0, tiled=False)  103 us
    pallas_call x1, Pallas kernels, inverse_parts(): pl.pallas_call(factor_kernel, out_shape=(half, half), in_specs=[pl.BlockS...  52.3 us
    ppermute x6, waiting for transfers between devices, shift_y(): return lax.ppermute(x, 'row', [(r, (r + 2 * k) % 8) for r in range(8)])  38.7 us
    pallas_call x1, Pallas kernels, update_slots(): pl.pallas_call(slot_kernel, out_shape=jax.ShapeDtypeStruct((12, B, 1024),...  25.9 us
    concatenate x1, other arithmetic, two_tiles(): jnp.concatenate([slices, more])  15.4 us
    ppermute x6, starting transfers between devices, shift_y(): return lax.ppermute(x, 'row', [(r, (r + 2 * k) % 8) for r in range(8)])  9.27 us
    pallas_call x1, Pallas kernels, solve_own(): pl.pallas_call(own_kernel, out_shape=jax.ShapeDtypeStruct((2, 1024, 1024)...  7.88 us
  transfers between devices with their start and end apart: 16, of which 7 were waited for; matrix products, arithmetic and copies ran while one was open for 1% of the time, Pallas kernels for 21%

profile of v1, /device:TPU:1, one launch (start us, length us, event | category | flops | bytes accessed | tf_op | source)
XLA Modules:
  0.0 286.4 jit_solution(1478283157321798073)
XLA Ops:
  7.2 0.8 copy.16
  11.6 1.7 constant_dynamic-slice_fusion
  13.3 3.8 %collective-permute-start.9 = (f32[128,1024]{1,0:T(8,128)}, f32[128,1024]{1,0:T(8,128)S(1)}, u32[]{:S(2)}, u32[]{:S(2)}) collective-permute-start(f32[128,1024]{1,0:T(8,128)} %refs_0_.1), channel_id=1, source_target_pairs={{0,128},{32,160},{64,192},{96,224},{128,0},{160,32},{192,64},{224,... | collective-permute-start | bytes 1572872 | tf_op jit(solution)/shard_map/ppermute | solution.py:192
  17.1 0.8 collective-permute-start.8
  17.9 1.4 collective-permute-start.2
  19.3 1.7 collective-permute-start.1
  23.3 1.1 bitcast_dynamic-update-slice_fusion.7
  24.4 27.8 %collective-permute-done = bf16[2,128,1024]{2,1,0:T(8,128)(2,1)S(1)} collective-permute-done((bf16[2,128,1024]{2,1,0:T(8,128)(2,1)}, bf16[2,128,1024]{2,1,0:T(8,128)(2,1)S(1)}, u32[]{:S(2)}, u32[]{:S(2)}) %collective-permute-start) | collective-permute-done | bytes 524320 | tf_op jit(solution)/shard_map/ppermute | solution.py:192
  52.7 1.6 collective-permute-start.7
  54.6 8.3 %collective-permute-done.1 = bf16[2,128,1024]{2,1,0:T(8,128)(2,1)S(1)} collective-permute-done((bf16[2,128,1024]{2,1,0:T(8,128)(2,1)}, bf16[2,128,1024]{2,1,0:T(8,128)(2,1)S(1)}, u32[]{:S(2)}, u32[]{:S(2)}) %collective-permute-start.1) | collective-permute-done | bytes 524320 | tf_op jit(solution)/shard_map/ppermute | solution.py:192
  62.9 1.5 collective-permute-start.5
  65.2 2.5 collective-permute-done.7.refs_1_
  67.8 0.8 collective-permute-start.13
  69.2 0.9 collective-permute-done.13.refs_7_
  70.1 0.7 collective-permute-done.12.refs_6_
  70.9 0.7 collective-permute-done.11.refs_5_
  71.6 52.3 %factor.1 = (bf16[1024,1024]{1,0:T(8,128)(2,1)S(1)}, bf16[1024,1024]{1,0:T(8,128)(2,1)S(1)}) custom-call(s32[8]{0:T(128)S(1)} %pad_add_fusion.1.ranks, f32[128,1024]{1,0:T(8,128)S(1)} %copy-done.1, f32[128,1024]{1,0:T(8,128)S(1)} %collective-permute-done.7.refs_1_, f32[128,1024]{1,0:T(8,128)S(1)} %collective-permute-done.8.refs_2_, ...), custom_call_target="tpu_custom_call" | custom-call | flops 20000000000 | bytes 100000000 | tf_op jit(solution)/shard_map/factor/pallas_call | solution.py:109
  124.0 7.9 %own.1 = bf16[2,1024,1024]{2,1,0:T(8,128)(2,1)S(1)} custom-call(s32[8]{0:T(128)S(1)} %pad_add_fusion.1.ranks, bf16[8,2,128,1024]{3,2,1,0:T(8,128)(2,1)S(1)} %bitcast_dynamic-update-slice_fusion.raw, bf16[1024,1024]{1,0:T(8,128)(2,1)S(1)} %get-tuple-element.47.high, bf16[1024,1024]{1,0:T(8,128)(2,1)S(1)} %get-tuple-element.48.low), custom_call_target="tpu_custom_call" | custom-call | flops 6000000000 | bytes 12000000 | tf_op jit(solution)/shard_map/own/pallas_call | solution.py:138
  131.9 2.1 copy-done.2
  133.9 0.8 constant_dynamic-slice_fusion.4
  134.8 144.7 %conditional.1 = (bf16[1,12,128,1024]{3,2,1,0:T(8,128)(2,1)}) conditional(s32[]{:T(128)} %convert_element_type.8, (bf16[1,12,128,1024]{3,2,1,0:T(8,128)(2,1)}, s32[3,12]{1,0:T(4,128)S(1)}, bf16[32,128,1024]{2,1,0:T(8,128)(2,1)}, bf16[1024,1024]{1,0:T(8,128)(2,1)}, bf16[1024,1024]{1,0:T(8,128)(2,1)}, ...), branch_computations={%region_2.3_spmd, %region_3.4_spmd} | conditional | flops 8008388608 | bytes 124168480 | solution.py:232
  135.5 102.7 %all-gather.3.cloned.1.call-done = bf16[32,128,1024]{2,1,0:T(8,128)(2,1)} async-done(((bf16[1,128,1024]{2,1,0:T(8,128)(2,1)}), bf16[32,128,1024]{2,1,0:T(8,128)(2,1)}) %all-gather.3.cloned.1.call-update) | async-done | bytes 8388624 | tf_op jit(solution)/shard_map/cond/branch_1_fun/all_gather | solution.py:229
  238.2 15.4 %pad_maximum_fusion.raw = bf16[64,128,1024]{2,1,0:T(8,128)(2,1)} fusion(bf16[32,128,1024]{2,1,0:T(8,128)(2,1)} %all-gather.3.cloned.1.call-done, bf16[32,128,1024]{2,1,0:T(8,128)(2,1)} %get-tuple-element.37), kind=kLoop, calls=%fused_computation.1 | loop fusion | flops 8388608 | bytes 33554432 | tf_op jit(solution)/shard_map/cond/branch_1_fun/concatenate | solution.py:230
  253.7 25.9 %slots.3 = bf16[12,128,1024]{2,1,0:T(8,128)(2,1)} custom-call(s32[3,12]{1,0:T(4,128)S(1)} %get-tuple-element.36.table, bf16[64,128,1024]{2,1,0:T(8,128)(2,1)} %pad_maximum_fusion.raw, bf16[1024,1024]{1,0:T(8,128)(2,1)S(1)} %copy-done.6, bf16[1024,1024]{1,0:T(8,128)(2,1)S(1)} %copy-done.8, bf16[2,1024,1024]{2,1,0:T(8,128)(2,1)S(1)} %copy-done.3, ...), custom_call_target="tpu_custom_call" | custom-call | flops 8000000000 | bytes 18000000 | tf_op jit(solution)/shard_map/cond/branch_1_fun/slots/pallas_call | solution.py:170
  (62 shorter events, 6.3 us)
Async XLA Ops:
  7.2 14.5 %copy-start = (s32[32,12]{0,1:T(8,128)S(1)}, s32[32,12]{0,1:T(8,128)}, u32[]{:S(2)}) copy-start(s32[32,12]{0,1:T(8,128)} %param.12) | copy-start | bytes 4612
  7.2 57.5 %copy-start.1 = (f32[128,1024]{1,0:T(8,128)S(1)}, f32[128,1024]{1,0:T(8,128)}, u32[]{:S(2)}) copy-start(f32[128,1024]{1,0:T(8,128)} %refs_0_.1) | copy-start | bytes 1572868
  7.2 127.6 %all-gather.5.cloned.1.call-start = ((), (), s32[]{:S(2)}) async-start(), calls=%async_computation.1 | async-start | bytes 8650752 | tf_op jit(solution)/shard_map/all_gather | solution.py:212
  13.3 39.4 %collective-permute-start.9 = (f32[128,1024]{1,0:T(8,128)}, f32[128,1024]{1,0:T(8,128)S(1)}, u32[]{:S(2)}, u32[]{:S(2)}) collective-permute-start(f32[128,1024]{1,0:T(8,128)} %refs_0_.1), channel_id=1, source_target_pairs={{0,128},{32,160},{64,192},{96,224},{128,0},{160,32},{192,64},{224,... | collective-permute-start | bytes 1572872 | tf_op jit(solution)/shard_map/ppermute | solution.py:192
  17.1 47.5 %collective-permute-start.8 = (f32[128,1024]{1,0:T(8,128)}, f32[128,1024]{1,0:T(8,128)S(1)}, u32[]{:S(2)}, u32[]{:S(2)}) collective-permute-start(f32[128,1024]{1,0:T(8,128)} %refs_0_.1), channel_id=1, source_target_pairs={{0,192},{32,224},{64,0},{96,32},{128,64},{160,96},{192,128},{224,1... | collective-permute-start | bytes 1572872 | tf_op jit(solution)/shard_map/ppermute | solution.py:192
  17.9 36.4 %collective-permute-start.2 = (bf16[2,128,1024]{2,1,0:T(8,128)(2,1)}, bf16[2,128,1024]{2,1,0:T(8,128)(2,1)S(1)}, u32[]{:S(2)}, u32[]{:S(2)}) collective-permute-start(bf16[2,128,1024]{2,1,0:T(8,128)(2,1)} %param.9), channel_id=1, source_target_pairs={{0,128},{32,160},{64,192},{96,224},{128,0},{160,32},{192,64},{224,... | collective-permute-start | bytes 1572872 | tf_op jit(solution)/shard_map/ppermute | solution.py:192
  19.3 43.6 %collective-permute-start.1 = (bf16[2,128,1024]{2,1,0:T(8,128)(2,1)}, bf16[2,128,1024]{2,1,0:T(8,128)(2,1)S(1)}, u32[]{:S(2)}, u32[]{:S(2)}) collective-permute-start(bf16[2,128,1024]{2,1,0:T(8,128)(2,1)} %param.9), channel_id=1, source_target_pairs={{0,192},{32,224},{64,0},{96,32},{128,64},{160,96},{192,128},{224,1... | collective-permute-start | bytes 1572872 | tf_op jit(solution)/shard_map/ppermute | solution.py:192
  21.0 31.2 %collective-permute-start = (bf16[2,128,1024]{2,1,0:T(8,128)(2,1)}, bf16[2,128,1024]{2,1,0:T(8,128)(2,1)S(1)}, u32[]{:S(2)}, u32[]{:S(2)}) collective-permute-start(bf16[2,128,1024]{2,1,0:T(8,128)(2,1)} %param.9), channel_id=1, source_target_pairs={{0,64},{32,96},{64,128},{96,160},{128,192},{160,224},{192,0},{224,... | collective-permute-start | bytes 1572872 | tf_op jit(solution)/shard_map/ppermute | solution.py:192
  52.2 12.3 %collective-permute-start.3 = (bf16[2,128,1024]{2,1,0:T(8,128)(2,1)}, bf16[2,128,1024]{2,1,0:T(8,128)(2,1)S(1)}, u32[]{:S(2)}, u32[]{:S(2)}) collective-permute-start(bf16[2,128,1024]{2,1,0:T(8,128)(2,1)} %param.9), channel_id=1, source_target_pairs={{0,32},{32,0},{64,96},{96,64},{128,160},{160,128},{192,224},{224,1... | collective-permute-start | bytes 1572872 | tf_op jit(solution)/shard_map/ppermute | solution.py:196
  52.7 15.0 %collective-permute-start.7 = (f32[128,1024]{1,0:T(8,128)}, f32[128,1024]{1,0:T(8,128)S(1)}, u32[]{:S(2)}, u32[]{:S(2)}) collective-permute-start(f32[128,1024]{1,0:T(8,128)} %refs_0_.1), channel_id=1, source_target_pairs={{0,64},{32,96},{64,128},{96,160},{128,192},{160,224},{192,0},{224,... | collective-permute-start | bytes 1572872 | tf_op jit(solution)/shard_map/ppermute | solution.py:192
  54.3 14.3 %collective-permute-start.4 = (bf16[2,128,1024]{2,1,0:T(8,128)(2,1)S(1)}, bf16[2,128,1024]{2,1,0:T(8,128)(2,1)S(1)}, u32[]{:S(2)}, u32[]{:S(2)}) collective-permute-start(bf16[2,128,1024]{2,1,0:T(8,128)(2,1)S(1)} %collective-permute-done), channel_id=1, source_target_pairs={{0,32},{32,0},{64,96},{96,64},{128,160},{160,128},{192,224},{224,1... | collective-permute-start | bytes 1572872 | tf_op jit(solution)/shard_map/ppermute | solution.py:196
  62.9 5.7 %collective-permute-start.5 = (bf16[2,128,1024]{2,1,0:T(8,128)(2,1)S(1)}, bf16[2,128,1024]{2,1,0:T(8,128)(2,1)S(1)}, u32[]{:S(2)}, u32[]{:S(2)}) collective-permute-start(bf16[2,128,1024]{2,1,0:T(8,128)(2,1)S(1)} %collective-permute-done.1), channel_id=1, source_target_pairs={{0,32},{32,0},{64,96},{96,64},{128,160},{160,128},{192,224},{224,1... | collective-permute-start | bytes 1572872 | tf_op jit(solution)/shard_map/ppermute | solution.py:196
  64.5 4.7 %collective-permute-start.6 = (bf16[2,128,1024]{2,1,0:T(8,128)(2,1)S(1)}, bf16[2,128,1024]{2,1,0:T(8,128)(2,1)S(1)}, u32[]{:S(2)}, u32[]{:S(2)}) collective-permute-start(bf16[2,128,1024]{2,1,0:T(8,128)(2,1)S(1)} %collective-permute-done.2), channel_id=1, source_target_pairs={{0,32},{32,0},{64,96},{96,64},{128,160},{160,128},{192,224},{224,1... | collective-permute-start | bytes 1572872 | tf_op jit(solution)/shard_map/ppermute | solution.py:196
  64.7 4.6 %collective-permute-start.10 = (f32[128,1024]{1,0:T(8,128)S(1)}, f32[128,1024]{1,0:T(8,128)S(1)}, u32[]{:S(2)}, u32[]{:S(2)}) collective-permute-start(f32[128,1024]{1,0:T(8,128)S(1)} %copy-done.1), channel_id=1, source_target_pairs={{0,32},{32,0},{64,96},{96,64},{128,160},{160,128},{192,224},{224,1... | collective-permute-start | bytes 1572872 | tf_op jit(solution)/shard_map/ppermute | solution.py:196
  67.8 2.3 collective-permute-start.13
  68.6 2.3 collective-permute-start.12
  68.6 3.0 %collective-permute-start.11 = (f32[128,1024]{1,0:T(8,128)S(1)}, f32[128,1024]{1,0:T(8,128)S(1)}, u32[]{:S(2)}, u32[]{:S(2)}) collective-permute-start(f32[128,1024]{1,0:T(8,128)S(1)} %collective-permute-done.7.refs_1_), channel_id=1, source_target_pairs={{0,32},{32,0},{64,96},{96,64},{128,160},{160,128},{192,224},{224,1... | collective-permute-start | bytes 1572872 | tf_op jit(solution)/shard_map/ppermute | solution.py:196
  123.9 7.9 %copy-start.5 = (bf16[1024,1024]{1,0:T(8,128)(2,1)}, bf16[1024,1024]{1,0:T(8,128)(2,1)S(1)}, u32[]{:S(2)}) copy-start(bf16[1024,1024]{1,0:T(8,128)(2,1)S(1)} %get-tuple-element.47.high) | copy-start | bytes 6291460
  124.0 10.8 %copy-start.9 = (bf16[2,128,1024]{2,1,0:T(8,128)(2,1)S(1)}, bf16[2,128,1024]{2,1,0:T(8,128)(2,1)}, u32[]{:S(2)}) copy-start(bf16[2,128,1024]{2,1,0:T(8,128)(2,1)} %param.9) | copy-start | bytes 1572868
  134.8 103.4 %all-gather.3.cloned.1.call-start = ((), (), s32[]{:S(2)}) async-start(), calls=%async_computation | async-start | bytes 8650752 | tf_op jit(solution)/shard_map/cond/branch_1_fun/all_gather | solution.py:229
  238.2 15.4 %copy-start.3 = (bf16[2,1024,1024]{2,1,0:T(8,128)(2,1)S(1)}, bf16[2,1024,1024]{2,1,0:T(8,128)(2,1)}, u32[]{:S(2)}) copy-start(bf16[2,1024,1024]{2,1,0:T(8,128)(2,1)} %get-tuple-element.41.tiles) | copy-start | bytes 12582916 | tf_op jit(solution)/shard_map/cond
  238.2 15.4 %copy-start.4 = (bf16[1,12,128,1024]{3,2,1,0:T(8,128)(2,1)S(1)}, bf16[1,12,128,1024]{3,2,1,0:T(8,128)(2,1)}, u32[]{:S(2)}) copy-start(bf16[1,12,128,1024]{3,2,1,0:T(8,128)(2,1)} %get-tuple-element.42) | copy-start | bytes 9437188 | tf_op jit(solution)/shard_map/cond
  238.2 15.4 %copy-start.6 = (bf16[1024,1024]{1,0:T(8,128)(2,1)S(1)}, bf16[1024,1024]{1,0:T(8,128)(2,1)}, u32[]{:S(2)}) copy-start(bf16[1024,1024]{1,0:T(8,128)(2,1)} %get-tuple-element.39.high) | copy-start | bytes 6291460 | tf_op jit(solution)/shard_map/cond
  238.2 15.4 %copy-start.8 = (bf16[1024,1024]{1,0:T(8,128)(2,1)S(1)}, bf16[1024,1024]{1,0:T(8,128)(2,1)}, u32[]{:S(2)}) copy-start(bf16[1024,1024]{1,0:T(8,128)(2,1)} %get-tuple-element.40.low) | copy-start | bytes 6291460 | tf_op jit(solution)/shard_map/cond
  (2 other events, 10.0 us)
Sparse Core Ops, SparseCore 0:
  13.4 101.9 all-gather.4
  138.8 99.4 all-gather.2

commit v2 on v1

--- a/solution.py
+++ b/solution.py
@@ -112,7 +112,7 @@
         in_specs=[pl.BlockSpec(memory_space=pltpu.SMEM)] + [vmem] * 8,
         out_specs=(vmem, vmem),
         scratch_shapes=[pltpu.VMEM((1024, 1024), F32), pltpu.VMEM((B, B), F32)],
-        compiler_params=pltpu.CompilerParams(vmem_limit_bytes=40 << 20),
+        compiler_params=pltpu.CompilerParams(vmem_limit_bytes=16 << 20),
         cost_estimate=pl.CostEstimate(flops=20_000_000_000, bytes_accessed=100_000_000, transcendentals=0),
         name="factor",
     )(ranks, *parts)
@@ -128,64 +128,94 @@
     return jnp.concatenate(pieces, axis=1)
 
 
-def own_kernel(ranks, raw, high, low, out):
-    solved = solve_rows(raw[...].reshape(2 * B, 1024), high, low)
-    out[...] = solved.reshape(2, B, 1024)
-
-
-def solve_own(ranks, raw, high, low):
-    whole = pl.BlockSpec((1024, 1024), lambda q, r: (0, 0))
+def own_kernel(ranks, *refs):
+    parts, (high, low, tiles, mine) = refs[:8], refs[8:]
+    for q in range(8):
+        solved = solve_rows(parts[q][...].reshape(2 * B, 1024), high, low).reshape(2, B, 1024)
+        tiles[:, pl.ds(pl.multiple_of(ranks[q] * B, B), B), :] = solved
+        if q == 0:
+            mine[...] = solved
+
+
+def solve_own(ranks, parts, high, low):
+    vmem = pl.BlockSpec(memory_space=pltpu.VMEM)
     return pl.pallas_call(
         own_kernel,
-        out_shape=jax.ShapeDtypeStruct((2, 1024, 1024), BF16),
-        grid_spec=pltpu.PrefetchScalarGridSpec(
-            num_scalar_prefetch=1,
-            grid=(8,),
-            in_specs=[pl.BlockSpec((None, 2, B, 1024), lambda q, r: (q, 0, 0, 0)), whole, whole],
-            out_specs=pl.BlockSpec((2, B, 1024), lambda q, r: (0, r[q], 0)),
-        ),
-        compiler_params=pltpu.CompilerParams(vmem_limit_bytes=32 << 20),
+        out_shape=(jax.ShapeDtypeStruct((2, 1024, 1024), BF16), jax.ShapeDtypeStruct((2, B, 1024), BF16)),
+        in_specs=[pl.BlockSpec(memory_space=pltpu.SMEM)] + [vmem] * 10,
+        out_specs=(vmem, vmem),
+        compiler_params=pltpu.CompilerParams(vmem_limit_bytes=8 << 20),
         cost_estimate=pl.CostEstimate(flops=6_000_000_000, bytes_accessed=12_000_000, transcendentals=0),
         name="own",
-    )(ranks, raw, high, low)
-
-
-def slot_kernel(table, raw, high, low, tiles, trailing, out):
-    s = pl.program_id(0)
-
-    @pl.when(table[2, s] > 0)
-    def _():
-        left = solve_rows(raw[...], high, low)
-        product = dot(left, tiles[table[1, s]], ((1,), (1,)))
-        out[...] = (trailing[...].astype(F32) - product).astype(BF16)
-
-    @pl.when(table[2, s] == 0)
-    def _():
-        out[...] = trailing[...]
-
-
-def update_slots(table, slices, high, low, tiles, trailing):
-    whole = pl.BlockSpec((1024, 1024), lambda s, t: (0, 0))
-    slot = pl.BlockSpec((None, B, 1024), lambda s, t: (s, 0, 0))
+    )(ranks, *parts, high, low)
+
+
+def slot_kernel(table, source, high, low, tiles, trailing, out, raw, new, left, in_sems, out_sems):
+    def rows(p):
+        return pl.ds(pl.multiple_of(p * B, B), B)
+
+    def raw_copy(p):
+        return pltpu.make_async_copy(source.at[table[1, p]], raw.at[rows(p)], in_sems.at[p])
+
+    def new_copy(p):
+        return pltpu.make_async_copy(new.at[rows(p)], out.at[table[0, p]], out_sems.at[p])
+
+    def subtract(p, first, b):
+        for n in range(0, 1024, 256):
+            product = dot(left[first * B:, :], tiles[b, n:n + 256, :], ((1,), (1,)))
+            for i in range(2 - first):
+                before = trailing[table[0, p + i], :, n:n + 256].astype(F32)
+                new[rows(p + i), n:n + 256] = (before - product[i * B:i * B + B, :]).astype(BF16)
+
+    for p in range(12):
+        raw_copy(p).start()
+
+    def pair(c, carry):
+        p = 2 * c
+        raw_copy(p).wait()
+        raw_copy(p + 1).wait()
+        live, both = table[3, p] > 0, table[3, p + 1] > 0
+
+        @pl.when(live)
+        def _():
+            block = pl.ds(pl.multiple_of(p * B, 2 * B), 2 * B)
+            for n in range(0, 1024, 256):
+                e = n + 256
+                some = raw[block, :e]
+                piece = dot(some, low[n:e, :e], ((1,), (1,))) + dot(some, high[n:e, :e], ((1,), (1,)))
+                left[:, n:e] = piece.astype(BF16)
+            subtract(p, 0, table[2, p])
+
+        @pl.when(jnp.logical_and(both, table[2, p + 1] != table[2, p]))
+        def _():
+            subtract(p + 1, 1, table[2, p + 1])
+
+        for i, used in enumerate((live, both)):
+            @pl.when(jnp.logical_not(used))
+            def _():
+                new[rows(p + i), :] = trailing[table[0, p + i]]
+
+            new_copy(p + i).start()
+        return carry
+
+    lax.fori_loop(0, 6, pair, 0)
+    for p in range(12):
+        new_copy(p).wait()
+
+
+def update_slots(table, source, high, low, tiles, trailing):
+    vmem, hbm = pl.BlockSpec(memory_space=pltpu.VMEM), pl.BlockSpec(memory_space=pltpu.HBM)
     return pl.pallas_call(
         slot_kernel,
         out_shape=jax.ShapeDtypeStruct((12, B, 1024), BF16),
-        grid_spec=pltpu.PrefetchScalarGridSpec(
-            num_scalar_prefetch=1,
-            grid=(12,),
-            in_specs=[
-                pl.BlockSpec((None, B, 1024), lambda s, t: (t[0, s], 0, 0)),
-                whole,
-                whole,
-                pl.BlockSpec((2, 1024, 1024), lambda s, t: (0, 0, 0)),
-                slot,
-            ],
-            out_specs=slot,
-        ),
-        compiler_params=pltpu.CompilerParams(vmem_limit_bytes=40 << 20),
-        cost_estimate=pl.CostEstimate(flops=8_000_000_000, bytes_accessed=18_000_000, transcendentals=0),
+        in_specs=[pl.BlockSpec(memory_space=pltpu.SMEM), hbm, vmem, vmem, vmem, vmem],
+        out_specs=hbm,
+        scratch_shapes=[pltpu.VMEM((12 * B, 1024), BF16)] * 2
+        + [pltpu.VMEM((2 * B, 1024), BF16), pltpu.SemaphoreType.DMA((12,)), pltpu.SemaphoreType.DMA((12,))],
+        compiler_params=pltpu.CompilerParams(vmem_limit_bytes=38 << 20),
+        cost_estimate=pl.CostEstimate(flops=8_000_000_000, bytes_accessed=12_000_000, transcendentals=0),
         name="slots",
-    )(table, slices, high, low, tiles, trailing)
+    )(table, source, high, low, tiles, trailing)
 
 
 def shift_y(x, k):
@@ -203,33 +233,29 @@
 
 def local(diag_block, panel, trailing, slot_rows, slot_cols):
     row, col = lax.axis_index("row"), lax.axis_index("col")
-    shifts = jnp.array([0, 1, 3, 2], jnp.int32)
-    ranks = jnp.concatenate([(row - 2 * shifts) % 8, ((row ^ 1) - 2 * shifts) % 8]).astype(jnp.int32)
-    wanted = jnp.any(slot_rows.reshape(1, -1) == jnp.arange(64, dtype=jnp.int32)[:, None], axis=1).reshape(32, 2)
-    both = wanted[:, 0] & wanted[:, 1]
-    first = jnp.where(wanted[:, 0], 0, 1)
-    mine = lax.dynamic_index_in_dim(panel, first[col], 0, keepdims=False)
-    slices = lax.all_gather(mine, "col", axis=0, tiled=False)
-
-    high, low = inverse_parts(ranks, row_parts(diag_block))
-    tiles = solve_own(ranks, jnp.stack(row_parts(panel)), high, low)
-    panel_factor = lax.dynamic_slice_in_dim(tiles, row * B, B, axis=1)
+    order = jnp.array([0, 1, 3, 2], jnp.int32)
+    ranks = jnp.concatenate([(row - 2 * order) % 8, ((row ^ 1) - 2 * order) % 8]).astype(jnp.int32)
+
+    source = lax.all_gather(panel, "col", axis=0, tiled=True)
+    diag_parts = row_parts(diag_block)
+    own, *diag_parts = lax.optimization_barrier((panel, *diag_parts))
+    own_parts = row_parts(own)
+    high, low = inverse_parts(ranks, diag_parts)
+
+    tiles, panel_factor = solve_own(ranks, own_parts, high, low)
 
     rows = lax.dynamic_index_in_dim(slot_rows, col, 0, keepdims=False)
     cols = lax.dynamic_index_in_dim(slot_cols, col, 0, keepdims=False)
     live = rows >= 0
-    owner = jnp.maximum(rows, 0) // 2
-    second = both[owner] & (rows % 2 == 1)
-    table = jnp.stack([owner + 32 * (second & live), cols, live.astype(jnp.int32)])
-
-    def one_tile(slices):
-        return update_slots(table, slices, high, low, tiles, trailing[0])
-
-    def two_tiles(slices):
-        more = lax.all_gather(panel[1], "col", axis=0, tiled=False)
-        return update_slots(table, jnp.concatenate([slices, more]), high, low, tiles, trailing[0])
-
-    updated = lax.cond(jnp.any(both), two_tiles, one_tile, slices)
+    key = jnp.where(live, cols, 2)
+    slot = jnp.arange(12, dtype=jnp.int32)
+    before = (key[None, :] < key[:, None]) | ((key[None, :] == key[:, None]) & (slot[None, :] < slot[:, None]))
+    place = jnp.sum(before.astype(jnp.int32), axis=1)
+    fields = jnp.stack([slot, jnp.maximum(rows, 0), cols, live.astype(jnp.int32)])
+    chosen = (place[None, :] == slot[:, None]).astype(jnp.int32)
+    table = jnp.sum(fields[:, None, :] * chosen[None, :, :], axis=2)
+
+    updated = update_slots(table, source, high, low, tiles, trailing[0])
     return (panel_factor, updated[None])
 
 

time: 287 us -> 181 us (0.63)
  waiting for transfers between devices: 144 us -> 36.1 us
  starting transfers between devices: 13.6 us -> 40 us
  other arithmetic: 17.6 us -> 2.97 us
  Pallas kernels: 86 us -> 74 us
  local copies, waits for them, and re-layouts: 8.54 us -> 13.3 us
    all_gather x2 -> x1, waiting for transfers between devices: 103 us -> 20 us  [local(): source = lax.all_gather(panel, 'col', axis=0, tiled=True)]
    ppermute x8, starting transfers between devices: 4.24 us -> 31.1 us  [other_core(): return lax.ppermute(x, 'row', [(r, r ^ 1) for r in range(8)])]
    ppermute x6, waiting for transfers between devices: 38.7 us -> 15.1 us  [shift_y(): return lax.ppermute(x, 'row', [(r, (r + 2 * k) % 8) for r in range(8)])]
    concatenate x2 -> x1, other arithmetic: 15.5 us -> 0.08 us  [local(): jnp.concatenate([(row - 2 * order) % 8, ((row ^ 1) - 2 * order) % 8])]
    pallas_call x1, Pallas kernels: 25.9 us -> 13.7 us  [update_slots(): pl.pallas_call(slot_kernel, out_shape=jax.ShapeDtypeStruct((12, B, 1024),...]
    unnamed x21 -> x22, local copies, waits for them, and re-layouts: 4.3 us -> 13.1 us
  transfers between devices with their start and end apart: 16 -> 15, of which waited for: 7 -> 6; matrix products, arithmetic and copies ran while one was open for 1% -> 2% of each run, Pallas kernels for 21% -> 33%
where the time goes in v2:
time: 181 us; the launch traced here: 180 us
  Pallas kernels  74 us (41%)
  starting transfers between devices  40 us (22%)
  waiting for transfers between devices  36.1 us (20%)
  between operations  14.2 us (8%)
  local copies, waits for them, and re-layouts  13.3 us (7%)
  other arithmetic  2.97 us (2%)
    pallas_call x1, Pallas kernels, inverse_parts(): pl.pallas_call(factor_kernel, out_shape=(half, half), in_specs=[pl.BlockS...  52.3 us
    ppermute x8, starting transfers between devices, other_core(): return lax.ppermute(x, 'row', [(r, r ^ 1) for r in range(8)])  31.1 us
    all_gather x1, waiting for transfers between devices, local(): source = lax.all_gather(panel, 'col', axis=0, tiled=True)  20 us
    ppermute x6, waiting for transfers between devices, shift_y(): return lax.ppermute(x, 'row', [(r, (r + 2 * k) % 8) for r in range(8)])  15.1 us
    pallas_call x1, Pallas kernels, update_slots(): pl.pallas_call(slot_kernel, out_shape=jax.ShapeDtypeStruct((12, B, 1024),...  13.7 us
    unnamed x22, local copies, waits for them, and re-layouts  13.1 us
    ppermute x6, starting transfers between devices, shift_y(): return lax.ppermute(x, 'row', [(r, (r + 2 * k) % 8) for r in range(8)])  8.81 us
    pallas_call x1, Pallas kernels, solve_own(): pl.pallas_call(own_kernel, out_shape=(jax.ShapeDtypeStruct((2, 1024, 1024...  7.96 us
  transfers between devices with their start and end apart: 15, of which 6 were waited for; matrix products, arithmetic and copies ran while one was open for 2% of the time, Pallas kernels for 33%

profile of v2, /device:TPU:1, one launch (start us, length us, event | category | flops | bytes accessed | tf_op | source)
XLA Modules:
  0.0 180.5 jit_solution(114343297643688796)
XLA Ops:
  7.9 2.2 %collective-permute-start = (f32[128,1024]{1,0:T(8,128)}, f32[128,1024]{1,0:T(8,128)S(1)}, u32[]{:S(2)}, u32[]{:S(2)}) collective-permute-start(f32[128,1024]{1,0:T(8,128)} %refs_0_), channel_id=1, source_target_pairs={{0,64},{32,96},{64,128},{96,160},{128,192},{160,224},{192,0},{224,... | collective-permute-start | bytes 1572872 | tf_op jit(solution)/shard_map/ppermute | solution.py:222
  10.1 1.5 collective-permute-start.1
  11.6 1.6 collective-permute-start.2
  13.2 1.5 collective-permute-start.3
  15.5 5.9 %collective-permute-done.refs_1_ = f32[128,1024]{1,0:T(8,128)S(1)} collective-permute-done((f32[128,1024]{1,0:T(8,128)}, f32[128,1024]{1,0:T(8,128)S(1)}, u32[]{:S(2)}, u32[]{:S(2)}) %collective-permute-start) | collective-permute-done | bytes 524320 | tf_op jit(solution)/shard_map/ppermute | solution.py:222
  21.4 3.3 %collective-permute-start.4 = (f32[128,1024]{1,0:T(8,128)S(1)}, f32[128,1024]{1,0:T(8,128)S(1)}, u32[]{:S(2)}, u32[]{:S(2)}) collective-permute-start(f32[128,1024]{1,0:T(8,128)S(1)} %collective-permute-done.refs_1_), channel_id=1, source_target_pairs={{0,32},{32,0},{64,96},{96,64},{128,160},{160,128},{192,224},{224,1... | collective-permute-start | bytes 1572872 | tf_op jit(solution)/shard_map/ppermute | solution.py:226
  24.6 10.7 %collective-permute-start.5 = (f32[128,1024]{1,0:T(8,128)S(1)}, f32[128,1024]{1,0:T(8,128)S(1)}, u32[]{:S(2)}, u32[]{:S(2)}) collective-permute-start(f32[128,1024]{1,0:T(8,128)S(1)} %collective-permute-done.1.refs_2_), channel_id=1, source_target_pairs={{0,32},{32,0},{64,96},{96,64},{128,160},{160,128},{192,224},{224,1... | collective-permute-start | bytes 1572872 | tf_op jit(solution)/shard_map/ppermute | solution.py:226
  35.5 1.5 collective-permute-start.6
  40.2 1.8 %collective-permute-start.8 = (bf16[2,128,1024]{2,1,0:T(8,128)(2,1)}, bf16[2,128,1024]{2,1,0:T(8,128)(2,1)}, u32[]{:S(2)}, u32[]{:S(2)}) collective-permute-start(bf16[2,128,1024]{2,1,0:T(8,128)(2,1)} %refs_0_.1), channel_id=1, source_target_pairs={{0,192},{32,224},{64,0},{96,32},{128,64},{160,96},{192,128},{224,1... | collective-permute-start | bytes 1572872 | tf_op jit(solution)/shard_map/ppermute | solution.py:222
  45.4 8.7 %collective-permute-done.7.refs_1_ = bf16[2,128,1024]{2,1,0:T(8,128)(2,1)} collective-permute-done((bf16[2,128,1024]{2,1,0:T(8,128)(2,1)}, bf16[2,128,1024]{2,1,0:T(8,128)(2,1)}, u32[]{:S(2)}, u32[]{:S(2)}) %collective-permute-start.7) | collective-permute-done | bytes 524320 | tf_op jit(solution)/shard_map/ppermute | solution.py:222
  54.0 1.2 collective-permute-start.11
  55.2 10.5 %collective-permute-start.12 = (bf16[2,128,1024]{2,1,0:T(8,128)(2,1)}, bf16[2,128,1024]{2,1,0:T(8,128)(2,1)S(1)}, u32[]{:S(2)}, u32[]{:S(2)}) collective-permute-start(bf16[2,128,1024]{2,1,0:T(8,128)(2,1)} %collective-permute-done.8.refs_2_), channel_id=1, source_target_pairs={{0,32},{32,0},{64,96},{96,64},{128,160},{160,128},{192,224},{224,1... | collective-permute-start | bytes 1572872 | tf_op jit(solution)/shard_map/ppermute | solution.py:226
  66.1 1.2 collective-permute-start.13
  68.4 1.2 copy-done.10
  69.6 52.3 %factor.1 = (bf16[1024,1024]{1,0:T(8,128)(2,1)S(1)}, bf16[1024,1024]{1,0:T(8,128)(2,1)S(1)}) custom-call(s32[8]{0:T(128)S(1)} %pad_add_fusion.1.ranks, f32[128,1024]{1,0:T(8,128)S(1)} %copy-done.8, f32[128,1024]{1,0:T(8,128)S(1)} %collective-permute-done.refs_1_, f32[128,1024]{1,0:T(8,128)S(1)} %collective-permute-done.1.refs_2_, ...), custom_call_target="tpu_custom_call" | custom-call | flops 20000000000 | bytes 100000000 | tf_op jit(solution)/shard_map/factor/pallas_call | solution.py:109
  122.0 8.0 %own.1 = (bf16[2,1024,1024]{2,1,0:T(8,128)(2,1)S(1)}, bf16[2,128,1024]{2,1,0:T(8,128)(2,1)}) custom-call(s32[8]{0:T(128)S(1)} %pad_add_fusion.1.ranks, bf16[2,128,1024]{2,1,0:T(8,128)(2,1)S(1)} %copy-done.7, bf16[2,128,1024]{2,1,0:T(8,128)(2,1)} %collective-permute-done.7.refs_1_, bf16[2,128,1024]{2,1,0:T(8,128)(2,1)} %collective-permute-done.8.refs_2_, ...), custom_call_target="tpu_custom_call" | custom-call | flops 6000000000 | bytes 12000000 | tf_op jit(solution)/shard_map/own/pallas_call | solution.py:142
  130.0 1.9 %copy-done = bf16[2,1024,1024]{2,1,0:T(8,128)(2,1)} copy-done((bf16[2,1024,1024]{2,1,0:T(8,128)(2,1)}, bf16[2,1024,1024]{2,1,0:T(8,128)(2,1)S(1)}, u32[]{:S(2)}) %copy-start) | copy-done | bytes 4194328
  131.9 1.3 copy-done.3
  133.3 1.3 copy-done.5
  134.6 20.0 %all-gather.2.cloned.1.call-done.source = bf16[64,128,1024]{2,1,0:T(8,128)(2,1)} async-done(((bf16[2,128,1024]{2,1,0:T(8,128)(2,1)}), bf16[64,128,1024]{2,1,0:T(8,128)(2,1)}) %all-gather.2.cloned.1.call-update) | async-done | bytes 16777232 | tf_op jit(solution)/shard_map/all_gather | solution.py:239
  154.5 2.2 %copy-done.1 = bf16[2,1024,1024]{2,1,0:T(8,128)(2,1)S(1)} copy-done((bf16[2,1024,1024]{2,1,0:T(8,128)(2,1)S(1)}, bf16[2,1024,1024]{2,1,0:T(8,128)(2,1)}, u32[]{:S(2)}) %copy-start.1) | copy-done | bytes 4194328
  156.7 1.6 copy-done.4
  158.3 1.6 copy-done.6
  159.9 13.7 %slots.1 = bf16[12,128,1024]{2,1,0:T(8,128)(2,1)} custom-call(s32[4,12]{1,0:T(4,128)S(1)} %copy.12.table, bf16[64,128,1024]{2,1,0:T(8,128)(2,1)} %all-gather.2.cloned.1.call-done.source, bf16[1024,1024]{1,0:T(8,128)(2,1)S(1)} %copy-done.4, bf16[1024,1024]{1,0:T(8,128)(2,1)S(1)} %copy-done.6, bf16[2,1024,1024]{2,1,0:T(8,128)(2,1)S(1)} %copy-done.1, ...), custom_call_target="tpu_custom_call" | custom-call | flops 8000000000 | bytes 12000000 | tf_op jit(solution)/shard_map/slots/pallas_call | solution.py:208
  (43 shorter events, 9.6 us)
Async XLA Ops:
  7.2 147.4 %all-gather.2.cloned.1.call-start = ((), (), s32[]{:S(2)}) async-start(), calls=%async_computation | async-start | bytes 17301504 | tf_op jit(solution)/shard_map/all_gather | solution.py:239
  7.9 13.5 %collective-permute-start = (f32[128,1024]{1,0:T(8,128)}, f32[128,1024]{1,0:T(8,128)S(1)}, u32[]{:S(2)}, u32[]{:S(2)}) collective-permute-start(f32[128,1024]{1,0:T(8,128)} %refs_0_), channel_id=1, source_target_pairs={{0,64},{32,96},{64,128},{96,160},{128,192},{160,224},{192,0},{224,... | collective-permute-start | bytes 1572872 | tf_op jit(solution)/shard_map/ppermute | solution.py:222
  10.1 14.5 %collective-permute-start.1 = (f32[128,1024]{1,0:T(8,128)}, f32[128,1024]{1,0:T(8,128)S(1)}, u32[]{:S(2)}, u32[]{:S(2)}) collective-permute-start(f32[128,1024]{1,0:T(8,128)} %refs_0_), channel_id=1, source_target_pairs={{0,192},{32,224},{64,0},{96,32},{128,64},{160,96},{192,128},{224,1... | collective-permute-start | bytes 1572872 | tf_op jit(solution)/shard_map/ppermute | solution.py:222
  11.6 23.9 %collective-permute-start.2 = (f32[128,1024]{1,0:T(8,128)}, f32[128,1024]{1,0:T(8,128)S(1)}, u32[]{:S(2)}, u32[]{:S(2)}) collective-permute-start(f32[128,1024]{1,0:T(8,128)} %refs_0_), channel_id=1, source_target_pairs={{0,128},{32,160},{64,192},{96,224},{128,0},{160,32},{192,64},{224,... | collective-permute-start | bytes 1572872 | tf_op jit(solution)/shard_map/ppermute | solution.py:222
  13.2 25.0 %collective-permute-start.3 = (f32[128,1024]{1,0:T(8,128)}, f32[128,1024]{1,0:T(8,128)S(1)}, u32[]{:S(2)}, u32[]{:S(2)}) collective-permute-start(f32[128,1024]{1,0:T(8,128)} %refs_0_), channel_id=1, source_target_pairs={{0,32},{32,0},{64,96},{96,64},{128,160},{160,128},{192,224},{224,1... | collective-permute-start | bytes 1572872 | tf_op jit(solution)/shard_map/ppermute | solution.py:226
  21.4 16.8 %collective-permute-start.4 = (f32[128,1024]{1,0:T(8,128)S(1)}, f32[128,1024]{1,0:T(8,128)S(1)}, u32[]{:S(2)}, u32[]{:S(2)}) collective-permute-start(f32[128,1024]{1,0:T(8,128)S(1)} %collective-permute-done.refs_1_), channel_id=1, source_target_pairs={{0,32},{32,0},{64,96},{96,64},{128,160},{160,128},{192,224},{224,1... | collective-permute-start | bytes 1572872 | tf_op jit(solution)/shard_map/ppermute | solution.py:226
  24.6 13.5 %collective-permute-start.5 = (f32[128,1024]{1,0:T(8,128)S(1)}, f32[128,1024]{1,0:T(8,128)S(1)}, u32[]{:S(2)}, u32[]{:S(2)}) collective-permute-start(f32[128,1024]{1,0:T(8,128)S(1)} %collective-permute-done.1.refs_2_), channel_id=1, source_target_pairs={{0,32},{32,0},{64,96},{96,64},{128,160},{160,128},{192,224},{224,1... | collective-permute-start | bytes 1572872 | tf_op jit(solution)/shard_map/ppermute | solution.py:226
  35.5 3.1 %collective-permute-start.6 = (f32[128,1024]{1,0:T(8,128)S(1)}, f32[128,1024]{1,0:T(8,128)S(1)}, u32[]{:S(2)}, u32[]{:S(2)}) collective-permute-start(f32[128,1024]{1,0:T(8,128)S(1)} %collective-permute-done.2.refs_3_), channel_id=1, source_target_pairs={{0,32},{32,0},{64,96},{96,64},{128,160},{160,128},{192,224},{224,1... | collective-permute-start | bytes 1572872 | tf_op jit(solution)/shard_map/ppermute | solution.py:226
  39.4 14.7 %collective-permute-start.7 = (bf16[2,128,1024]{2,1,0:T(8,128)(2,1)}, bf16[2,128,1024]{2,1,0:T(8,128)(2,1)}, u32[]{:S(2)}, u32[]{:S(2)}) collective-permute-start(bf16[2,128,1024]{2,1,0:T(8,128)(2,1)} %refs_0_.1), channel_id=1, source_target_pairs={{0,64},{32,96},{64,128},{96,160},{128,192},{160,224},{192,0},{224,... | collective-permute-start | bytes 1572872 | tf_op jit(solution)/shard_map/ppermute | solution.py:222
  40.2 15.0 %collective-permute-start.8 = (bf16[2,128,1024]{2,1,0:T(8,128)(2,1)}, bf16[2,128,1024]{2,1,0:T(8,128)(2,1)}, u32[]{:S(2)}, u32[]{:S(2)}) collective-permute-start(bf16[2,128,1024]{2,1,0:T(8,128)(2,1)} %refs_0_.1), channel_id=1, source_target_pairs={{0,192},{32,224},{64,0},{96,32},{128,64},{160,96},{192,128},{224,1... | collective-permute-start | bytes 1572872 | tf_op jit(solution)/shard_map/ppermute | solution.py:222
  42.0 24.1 %collective-permute-start.9 = (bf16[2,128,1024]{2,1,0:T(8,128)(2,1)}, bf16[2,128,1024]{2,1,0:T(8,128)(2,1)}, u32[]{:S(2)}, u32[]{:S(2)}) collective-permute-start(bf16[2,128,1024]{2,1,0:T(8,128)(2,1)} %refs_0_.1), channel_id=1, source_target_pairs={{0,128},{32,160},{64,192},{96,224},{128,0},{160,32},{192,64},{224,... | collective-permute-start | bytes 1572872 | tf_op jit(solution)/shard_map/ppermute | solution.py:222
  44.2 77.8 %copy-start.7 = (bf16[2,128,1024]{2,1,0:T(8,128)(2,1)S(1)}, bf16[2,128,1024]{2,1,0:T(8,128)(2,1)}, u32[]{:S(2)}) copy-start(bf16[2,128,1024]{2,1,0:T(8,128)(2,1)} %refs_0_.1) | copy-start | bytes 1572868
  44.2 77.8 %collective-permute-start.10 = (bf16[2,128,1024]{2,1,0:T(8,128)(2,1)}, bf16[2,128,1024]{2,1,0:T(8,128)(2,1)S(1)}, u32[]{:S(2)}, u32[]{:S(2)}) collective-permute-start(bf16[2,128,1024]{2,1,0:T(8,128)(2,1)} %refs_0_.1), channel_id=1, source_target_pairs={{0,32},{32,0},{64,96},{96,64},{128,160},{160,128},{192,224},{224,1... | collective-permute-start | bytes 1572872 | tf_op jit(solution)/shard_map/ppermute | solution.py:226
  54.0 67.9 %collective-permute-start.11 = (bf16[2,128,1024]{2,1,0:T(8,128)(2,1)}, bf16[2,128,1024]{2,1,0:T(8,128)(2,1)S(1)}, u32[]{:S(2)}, u32[]{:S(2)}) collective-permute-start(bf16[2,128,1024]{2,1,0:T(8,128)(2,1)} %collective-permute-done.7.refs_1_), channel_id=1, source_target_pairs={{0,32},{32,0},{64,96},{96,64},{128,160},{160,128},{192,224},{224,1... | collective-permute-start | bytes 1572872 | tf_op jit(solution)/shard_map/ppermute | solution.py:226
  55.2 66.7 %collective-permute-start.12 = (bf16[2,128,1024]{2,1,0:T(8,128)(2,1)}, bf16[2,128,1024]{2,1,0:T(8,128)(2,1)S(1)}, u32[]{:S(2)}, u32[]{:S(2)}) collective-permute-start(bf16[2,128,1024]{2,1,0:T(8,128)(2,1)} %collective-permute-done.8.refs_2_), channel_id=1, source_target_pairs={{0,32},{32,0},{64,96},{96,64},{128,160},{160,128},{192,224},{224,1... | collective-permute-start | bytes 1572872 | tf_op jit(solution)/shard_map/ppermute | solution.py:226
  66.1 55.9 %collective-permute-start.13 = (bf16[2,128,1024]{2,1,0:T(8,128)(2,1)}, bf16[2,128,1024]{2,1,0:T(8,128)(2,1)S(1)}, u32[]{:S(2)}, u32[]{:S(2)}) collective-permute-start(bf16[2,128,1024]{2,1,0:T(8,128)(2,1)} %collective-permute-done.9.refs_3_), channel_id=1, source_target_pairs={{0,32},{32,0},{64,96},{96,64},{128,160},{160,128},{192,224},{224,1... | collective-permute-start | bytes 1572872 | tf_op jit(solution)/shard_map/ppermute | solution.py:226
  68.4 1.2 copy-start.10
  122.0 32.5 %copy-start.2 = (bf16[1,12,128,1024]{3,2,1,0:T(8,128)(2,1)S(1)}, bf16[1,12,128,1024]{3,2,1,0:T(8,128)(2,1)}, u32[]{:S(2)}) copy-start(bf16[1,12,128,1024]{3,2,1,0:T(8,128)(2,1)} %param.8) | copy-start | bytes 9437188
  130.0 1.9 %copy-start = (bf16[2,1024,1024]{2,1,0:T(8,128)(2,1)}, bf16[2,1024,1024]{2,1,0:T(8,128)(2,1)S(1)}, u32[]{:S(2)}) copy-start(bf16[2,1024,1024]{2,1,0:T(8,128)(2,1)S(1)} %get-tuple-element.27.tiles) | copy-start | bytes 12582916
  131.9 1.3 copy-start.3
  133.3 1.3 copy-start.5
  154.5 2.2 %copy-start.1 = (bf16[2,1024,1024]{2,1,0:T(8,128)(2,1)S(1)}, bf16[2,1024,1024]{2,1,0:T(8,128)(2,1)}, u32[]{:S(2)}) copy-start(bf16[2,1024,1024]{2,1,0:T(8,128)(2,1)} %copy-done) | copy-start | bytes 12582916
  156.7 1.6 copy-start.4
  158.3 1.6 copy-start.6
  (2 other events, 1.9 us)
Sparse Core Ops, SparseCore 0:
  10.6 143.9 all-gather.1
